TPU v7x, 32 devices: a whole 2x2x4 slice. The times are simulated.
32 devices in a mesh: row: 4 (over y, x), col: 8 (over z, core).
Axes of the slice: x: 2, y: 2, z: 4, core: 2. Of those that a mesh axis runs over, the one named last changes fastest.
Arguments:
- velocities: bfloat16 [1024, 30720], P(None, 'row'), may hold values from -60 to 60, as said below
- modes_panel: bfloat16 [30720, 4096], P('row', 'col'), may hold values from -1 to 1
- atom_slot: int32 [10240], P('row'), may hold values from 0 to 2559, as said below
- lag_offsets: int32 [8], replicated, may hold values from 0 to 256, as said below
Outputs:
- correlations: float32 [8, 4096, 4096], P(None, 'row', 'col')
Inputs may be any that keep to these rules, and one draw needn't show every extreme that they name: `velocities`: every snapshot row has its own scale. Within each aligned block of 2560 atoms, atom_slot is a permutation of 0 to 2559. `lag_offsets`: one of the lags equals 256.
All inputs are finite; a program needn't handle non-finite values.
Results may differ from a plain program's by a relative error of at most 0.0041.
Values may be sent and summed in bfloat16 or wider, within the bound.
No kernel may reach another device: no remote copies, remote signals or barrier semaphores. Data moves between devices by JAX's collectives and lax.ppermute only.
A program may use at most 128 MiB of HBM per device.

v0:
```python
import jax
import jax.numpy as jnp
from jax import lax
from jax.sharding import PartitionSpec as P

M = 4096
LAGS = 8
MAXLAG = 256
epsilon = 1e-06


def from_root(block, axis, owner):
    block = jnp.where(lax.axis_index(axis) == owner, block, jnp.zeros_like(block))
    return lax.psum(block, axis)


def reorder(modes_panel, atom_slot):
    per_atom = modes_panel.reshape(atom_slot.shape[0], 3, modes_panel.shape[1])
    return jnp.take(per_atom, atom_slot, axis=0).reshape(modes_panel.shape)


def correlate(row_modes, column_modes, lag_offsets):
    snapshots = column_modes.shape[0]
    padded = jnp.concatenate(
        [column_modes, jnp.zeros((MAXLAG, column_modes.shape[1]), jnp.bfloat16)], axis=0
    )
    results = []
    for number in range(LAGS):
        offset = lag_offsets[number]
        shifted = lax.dynamic_slice_in_dim(padded, offset, snapshots, 0)
        product = lax.dot_general(
            row_modes, shifted, (((0,), (0,)), ((), ())), preferred_element_type=jnp.float32
        )
        results.append(product * lax.rsqrt((snapshots - offset).astype(jnp.float32)))
    return jnp.stack(results)


def local(velocities, modes_panel, atom_slot, lag_offsets):
    panel = reorder(modes_panel, atom_slot)
    row_count = lax.axis_size("row")
    col_count = lax.axis_size("col")
    partial_terms = jnp.dot(velocities, panel, preferred_element_type=jnp.float32)
    projected = lax.psum(partial_terms, "row")
    energy = lax.psum(jnp.sum(projected * projected, axis=1), "col")
    column_modes = (projected * lax.rsqrt(energy / M + epsilon)[:, None]).astype(jnp.bfloat16)
    owners = col_count // row_count
    pieces = [
        from_root(column_modes, "col", lax.axis_index("row") * owners + owner)
        for owner in range(owners)
    ]
    row_modes = jnp.concatenate(pieces, axis=1)
    return correlate(row_modes, column_modes, lag_offsets)


def solution(mesh):
    return jax.shard_map(
        local,
        mesh=mesh,
        in_specs=(P(None, "row"), P("row", "col"), P("row"), P()),
        out_specs=P(None, "row", "col"),
        check_vma=False,
    )
```

profile of v0, /device:TPU:0, one launch (start us, length us, event | category | flops | bytes accessed | tf_op | source)
XLA Modules:
  0.0 267.6 jit_solution(14538257471376262001)
XLA Ops:
  6.5 0.7 compare_select_fusion
  7.2 0.7 compare_and_fusion
  8.0 20.7 %reshape.12 = bf16[2560,3,512]{2,1,0:T(4,128)(2,1)} reshape(bf16[7680,512]{1,0:T(8,128)(2,1)} %param.5) | data formatting | bytes 15728640 | tf_op jit(solution)/shard_map/reshape | solution.py:18
  28.7 17.1 %gather_fusion = bf16[2560,3,512]{2,1,0:T(4,128)(2,1)} fusion(bf16[2560,3,512]{2,1,0:T(4,128)(2,1)} %reshape.12, s32[3072]{0:T(1024)S(1)} %pad_clamp_fusion), kind=kCustom, calls=%fused_computation | custom fusion | bytes 15738880 | tf_op jit(solution)/shard_map/jit(_take)/gather | solution.py:19
  45.9 20.0 %gather.7 = bf16[7680,512]{1,0:T(8,128)(2,1)} reshape(bf16[2560,3,512]{2,1,0:T(4,128)(2,1)} %gather_fusion) | data formatting | bytes 15728640 | tf_op jit(solution)/shard_map/jit(_take)/gather | solution.py:19
  65.9 1.3 broadcast_in_dim.18
  67.2 1.1 broadcast_in_dim.19
  68.3 16.5 %fusion.4 = f32[1024,512]{0,1:T(8,128)} fusion(bf16[1024,7680]{1,0:T(8,128)(2,1)} %param.4, bf16[7680,512]{1,0:T(8,128)(2,1)} %gather.7, pred[7680]{0:T(1024)(128)(4,1)S(1)} %broadcast_in_dim.19), kind=kOutput, calls=%fused_computation.15 | convolution fusion | flops 8056995840 | bytes 25697792 | tf_op jit(solution)/shard_map/dot_general | solution.py:42
  84.9 72.3 %all-reduce.5.cloned.1.call-done = f32[1024,512]{0,1:T(8,128)} async-done(((f32[1024,512]{0,1:T(8,128)}), f32[1024,512]{0,1:T(8,128)}) %all-reduce.5.cloned.1.call-update) | async-done | bytes 2097168 | tf_op jit(solution)/shard_map/psum | solution.py:43
  157.2 1.9 multiply_reduce_fusion
  159.1 16.4 %psum.29 = f32[1024]{0:T(1024)S(1)} all-reduce(f32[1024]{0:T(1024)S(1)} %multiply_reduce_fusion), channel_id=1, replica_groups=mesh['row'=4,'col'=8] {'col'}, use_global_device_ids=true, to_apply=%region_2.3 | all-reduce | flops 1024 | bytes 8192 | tf_op jit(solution)/shard_map/psum | solution.py:44
  175.5 1.4 broadcast_select_fusion
  176.9 1.1 broadcast_select_fusion.1
  198.4 42.2 %all-reduce.7.cloned.1.call-done = (bf16[1024,512]{0,1:T(8,128)(2,1)}, bf16[1024,512]{0,1:T(8,128)(2,1)}) async-done(((bf16[1024,512]{0,1:T(8,128)(2,1)}, bf16[1024,512]{0,1:T(8,128)(2,1)}), (bf16[1024,512]{0,1:T(8,128)(2,1)}, bf16[1024,512]{0,1:T(8,128)(2,1)})) %all-reduce.7.cloned.1.call-update) | async-done | bytes 2097168 | tf_op jit(solution)/shard_map/psum | solution.py:14
  240.6 1.4 constant_dynamic-update-slice_fusion.1
  242.2 1.4 bitcast_dynamic-update-slice_fusion.7
  243.6 1.4 bitcast_dynamic-update-slice_fusion.6
  245.0 1.4 bitcast_dynamic-update-slice_fusion.5
  246.4 1.4 bitcast_dynamic-update-slice_fusion.4
  247.8 1.4 bitcast_dynamic-update-slice_fusion.3
  249.1 1.4 bitcast_dynamic-update-slice_fusion.2
  250.5 1.4 bitcast_dynamic-update-slice_fusion.1
  251.9 6.2 %copy-done.3 = f32[8,1024,512]{2,1,0:T(8,128)} copy-done((f32[8,1024,512]{2,1,0:T(8,128)}, f32[8,1024,512]{2,1,0:T(8,128)S(1)}, u32[]{:S(2)}) %copy-start.3) | copy-done | bytes 16777240
  258.1 2.7 %bitcast_dynamic-update-slice_fusion = f32[8,1024,512]{2,1,0:T(8,128)} fusion(f32[8,1024,512]{2,1,0:T(8,128)} %copy-done.3, bf16[1024,1024]{0,1:T(8,128)(2,1)S(1)} %constant_dynamic-update-slice_fusion, s32[]{:T(128)S(6)} %select_n.61, bf16[1024,512]{0,1:T(8,128)(2,1)S(1)} %get-tuple-element.8, f32[]{:T(128)S(6)} %rsqrt.35), kind=kOutput, calls=%fused_computation.5 | convolution fusion | flops 1074266112 | bytes 5242888 | tf_op jit(solution)/shard_map/dot_general | solution.py:31
  (15 shorter events, 1.0 us)
Async XLA Ops:
  6.5 150.7 %all-reduce.5.cloned.1.call-start = ((), (), s32[]{:S(2)}) async-start(), calls=%async_computation | async-start | bytes 4194304 | tf_op jit(solution)/shard_map/psum | solution.py:43
  84.9 155.8 %all-reduce.7.cloned.1.call-start = ((), (), s32[]{:S(2)}) async-start(), calls=%async_computation.1 | async-start | bytes 4194304 | tf_op jit(solution)/shard_map/psum | solution.py:14
  157.2 18.3 %copy-start = (f32[1024,512]{0,1:T(8,128)S(1)}, f32[1024,512]{0,1:T(8,128)}, u32[]{:S(2)}) copy-start(f32[1024,512]{0,1:T(8,128)} %all-reduce.5.cloned.1.call-done) | copy-start | bytes 6291460
  176.9 1.1 copy-start.2
  240.6 1.5 copy-start.1
  251.9 6.2 %copy-start.3 = (f32[8,1024,512]{2,1,0:T(8,128)}, f32[8,1024,512]{2,1,0:T(8,128)S(1)}, u32[]{:S(2)}) copy-start(f32[8,1024,512]{2,1,0:T(8,128)S(1)} %bitcast_dynamic-update-slice_fusion.1) | copy-start | bytes 50331652
Sparse Core Ops, SparseCore 0:
  85.0 72.1 all-reduce.4
  178.1 62.4 all-reduce.6
where the time goes:
time: 269 us; the launch traced here: 268 us
  waiting for transfers between devices  115 us (43%)
  local copies, waits for them, and re-layouts  68.8 us (26%)
  between operations  33.2 us (12%)
  matrix products  28.9 us (11%)
  blocking collectives  16.4 us (6%)
  other arithmetic  5.85 us (2%)
    psum x1, waiting for transfers between devices, local(): projected = lax.psum(partial_terms, 'row')  72.3 us
    psum x1, waiting for transfers between devices, from_root(): return lax.psum(block, axis)  42.2 us
    gather x2, local copies, waits for them, and re-layouts, reorder(): return jnp.take(per_atom, atom_slot, axis=0).reshape(modes_panel.shape)  37.2 us
    reshape x1, local copies, waits for them, and re-layouts, reorder(): per_atom = modes_panel.reshape(atom_slot.shape[0], 3, modes_panel.shape[1])  20.7 us
    dot_general x1, matrix products, local(): jnp.dot(velocities, panel, preferred_element_type=jnp.float32)  16.5 us
    psum x1, blocking collectives, local(): energy = lax.psum(jnp.sum(projected * projected, axis=1), 'col')  16.4 us
    dot_general x8, matrix products, correlate(): lax.dot_general(row_modes, shifted, (((0,), (0,)), ((), ())), preferred_e...  12.3 us
    unnamed x9, local copies, waits for them, and re-layouts  7.7 us
  transfers between devices with their start and end apart: 2, of which 2 were waited for; matrix products, arithmetic and copies ran while one was open for 0% of the time, Pallas kernels for 0%

commit v1 on v0

--- a/solution.py
+++ b/solution.py
@@ -1,12 +1,27 @@
+import functools
 import jax
 import jax.numpy as jnp
 from jax import lax
 from jax.sharding import PartitionSpec as P
+from jax.lax import axis_size, ppermute
 
 M = 4096
 LAGS = 8
 MAXLAG = 256
 epsilon = 1e-06
+
+
+def patches_store(incoming_x, chip_axis):
+    full_n = axis_size(chip_axis)
+    reached, now = (incoming_x, 0)
+    while 1 << now < full_n:
+        raw_out = ppermute(reached, chip_axis, [(ix, ix ^ 1 << now) for ix in range(full_n)])
+        reached = reached + raw_out
+        now = now + 1
+    return reached
+
+
+_see_sums_all = functools.partial(patches_store, chip_axis="row")
 
 
 def from_root(block, axis, owner):
@@ -40,7 +55,7 @@
     row_count = lax.axis_size("row")
     col_count = lax.axis_size("col")
     partial_terms = jnp.dot(velocities, panel, preferred_element_type=jnp.float32)
-    projected = lax.psum(partial_terms, "row")
+    projected = _see_sums_all(partial_terms)
     energy = lax.psum(jnp.sum(projected * projected, axis=1), "col")
     column_modes = (projected * lax.rsqrt(energy / M + epsilon)[:, None]).astype(jnp.bfloat16)
     owners = col_count // row_count

time: 269 us -> 294 us (1.093)
  waiting for transfers between devices: 115 us -> 134 us
  starting transfers between devices: 0.04 us -> 4.87 us
  other arithmetic: 5.85 us -> 9.27 us
    ppermute x0 -> x2, waiting for transfers between devices: none -> 90.8 us  [patches_store(): ppermute(reached, chip_axis, [(ix, ix ^ 1 << now) for ix in range(full_n)])]
    psum x1 -> x0, waiting for transfers between devices: 72.3 us -> none  [local(): projected = lax.psum(partial_terms, 'row')]
    ppermute x0 -> x2, starting transfers between devices: none -> 4.86 us  [patches_store(): ppermute(reached, chip_axis, [(ix, ix ^ 1 << now) for ix in range(full_n)])]
    unnamed x9 -> x7, local copies, waits for them, and re-layouts: 7.7 us -> 7.7 us
  transfers between devices with their start and end apart: 2 -> 3, of which waited for: 2 -> 3; matrix products, arithmetic and copies ran while one was open for 0% -> 0% of each run, Pallas kernels for 0% -> 0%
where the time goes in v1:
time: 294 us; the launch traced here: 293 us
  waiting for transfers between devices  134 us (46%)
  local copies, waits for them, and re-layouts  68.7 us (23%)
  between operations  33.5 us (11%)
  matrix products  27.7 us (9%)
  blocking collectives  15 us (5%)
  other arithmetic  9.27 us (3%)
  starting transfers between devices  4.87 us (2%)
    ppermute x2, waiting for transfers between devices, patches_store(): ppermute(reached, chip_axis, [(ix, ix ^ 1 << now) for ix in range(full_n)])  90.8 us
    psum x1, waiting for transfers between devices, from_root(): return lax.psum(block, axis)  43 us
    gather x2, local copies, waits for them, and re-layouts, reorder(): return jnp.take(per_atom, atom_slot, axis=0).reshape(modes_panel.shape)  37.2 us
    reshape x1, local copies, waits for them, and re-layouts, reorder(): per_atom = modes_panel.reshape(atom_slot.shape[0], 3, modes_panel.shape[1])  20.7 us
    dot_general x1, matrix products, local(): jnp.dot(velocities, panel, preferred_element_type=jnp.float32)  15.3 us
    psum x1, blocking collectives, local(): energy = lax.psum(jnp.sum(projected * projected, axis=1), 'col')  15 us
    dot_general x8, matrix products, correlate(): lax.dot_general(row_modes, shifted, (((0,), (0,)), ((), ())), preferred_e...  12.3 us
    unnamed x7, local copies, waits for them, and re-layouts  7.7 us
  transfers between devices with their start and end apart: 3, of which 3 were waited for; matrix products, arithmetic and copies ran while one was open for 0% of the time, Pallas kernels for 0%

profile of v1, /device:TPU:0, one launch (start us, length us, event | category | flops | bytes accessed | tf_op | source)
XLA Modules:
  0.0 292.8 jit_solution(14202692663391169260)
XLA Ops:
  8.0 20.7 %reshape.12 = bf16[2560,3,512]{2,1,0:T(4,128)(2,1)} reshape(bf16[7680,512]{1,0:T(8,128)(2,1)} %param.5) | data formatting | bytes 15728640 | tf_op jit(solution)/shard_map/reshape | solution.py:33
  28.7 17.1 %gather_fusion = bf16[2560,3,512]{2,1,0:T(4,128)(2,1)} fusion(bf16[2560,3,512]{2,1,0:T(4,128)(2,1)} %reshape.12, s32[3072]{0:T(1024)S(1)} %pad_clamp_fusion), kind=kCustom, calls=%fused_computation | custom fusion | bytes 15738880 | tf_op jit(solution)/shard_map/jit(_take)/gather | solution.py:34
  45.8 20.0 %gather.7 = bf16[7680,512]{1,0:T(8,128)(2,1)} reshape(bf16[2560,3,512]{2,1,0:T(4,128)(2,1)} %gather_fusion) | data formatting | bytes 15728640 | tf_op jit(solution)/shard_map/jit(_take)/gather | solution.py:34
  65.9 1.3 broadcast_in_dim.18
  67.2 1.1 broadcast_in_dim.19
  68.3 15.3 %fusion.4 = f32[1024,512]{0,1:T(8,128)S(1)} fusion(bf16[1024,7680]{1,0:T(8,128)(2,1)} %param.4, bf16[7680,512]{1,0:T(8,128)(2,1)} %gather.7, pred[7680]{0:T(1024)(128)(4,1)S(1)} %broadcast_in_dim.19), kind=kOutput, calls=%fused_computation.15 | convolution fusion | flops 8056995840 | bytes 25697792 | tf_op jit(solution)/shard_map/dot_general | solution.py:57
  83.6 3.0 %collective-permute-start = (f32[1024,512]{0,1:T(8,128)S(1)}, f32[1024,512]{0,1:T(8,128)S(1)}, u32[]{:S(2)}, u32[]{:S(2)}) collective-permute-start(f32[1024,512]{0,1:T(8,128)S(1)} %fusion.4), channel_id=1, source_target_pairs={{0,8},{8,0},{16,24},{24,16},{1,9},{9,1},{17,25},{25,17},{2,10},{10... | collective-permute-start | bytes 6291464 | tf_op jit(solution)/shard_map/ppermute | solution.py:18
  86.6 45.6 %collective-permute-done = f32[1024,512]{0,1:T(8,128)S(1)} collective-permute-done((f32[1024,512]{0,1:T(8,128)S(1)}, f32[1024,512]{0,1:T(8,128)S(1)}, u32[]{:S(2)}, u32[]{:S(2)}) %collective-permute-start) | collective-permute-done | bytes 2097184 | tf_op jit(solution)/shard_map/ppermute | solution.py:18
  132.7 1.8 collective-permute-start.1
  134.5 45.1 %collective-permute-done.1 = f32[1024,512]{0,1:T(8,128)} collective-permute-done((f32[1024,512]{0,1:T(8,128)S(1)}, f32[1024,512]{0,1:T(8,128)}, u32[]{:S(2)}, u32[]{:S(2)}) %collective-permute-start.1) | collective-permute-done | bytes 2097184 | tf_op jit(solution)/shard_map/ppermute | solution.py:18
  179.6 3.4 %multiply_reduce_fusion = (f32[1024]{0:T(1024)S(1)}, f32[1024,512]{0,1:T(8,128)}) fusion(f32[1024,512]{0,1:T(8,128)S(1)} %add.57, f32[1024,512]{0,1:T(8,128)} %collective-permute-done.1), kind=kLoop, calls=%fused_computation.14 | loop fusion | flops 1571840 | bytes 6295552 | tf_op jit(solution)/shard_map/reduce_sum | solution.py:59
  183.0 15.0 %psum.21 = f32[1024]{0:T(1024)S(1)} all-reduce(f32[1024]{0:T(1024)S(1)} %get-tuple-element.9), channel_id=1, replica_groups=mesh['row'=4,'col'=8] {'col'}, use_global_device_ids=true, to_apply=%region_1.2 | all-reduce | flops 1024 | bytes 8192 | tf_op jit(solution)/shard_map/psum | solution.py:59
  198.1 3.0 %broadcast_select_fusion = (bf16[1024,512]{0,1:T(8,128)(2,1)}, bf16[1024,512]{0,1:T(8,128)(2,1)S(1)}) fusion(pred[]{:T(512)S(6)} %eq.7, f32[1024,512]{0,1:T(8,128)} %get-tuple-element.10, f32[1024]{0:T(1024)S(1)} %add_rsqrt_fusion), kind=kLoop, calls=%fused_computation.24 | loop fusion | flops 1572864 | bytes 4198401 | tf_op jit(solution)/shard_map/jit(_where)/select_n | solution.py:28
  222.8 43.0 %all-reduce.4.cloned.1.call-done = (bf16[1024,512]{0,1:T(8,128)(2,1)}, bf16[1024,512]{0,1:T(8,128)(2,1)}) async-done(((bf16[1024,512]{0,1:T(8,128)(2,1)}, bf16[1024,512]{0,1:T(8,128)(2,1)}), (bf16[1024,512]{0,1:T(8,128)(2,1)}, bf16[1024,512]{0,1:T(8,128)(2,1)})) %all-reduce.4.cloned.1.call-update) | async-done | bytes 2097168 | tf_op jit(solution)/shard_map/psum | solution.py:29
  265.8 1.4 constant_dynamic-update-slice_fusion.1
  267.4 1.4 bitcast_dynamic-update-slice_fusion.7
  268.8 1.4 bitcast_dynamic-update-slice_fusion.6
  270.2 1.4 bitcast_dynamic-update-slice_fusion.5
  271.5 1.4 bitcast_dynamic-update-slice_fusion.4
  272.9 1.4 bitcast_dynamic-update-slice_fusion.3
  274.3 1.4 bitcast_dynamic-update-slice_fusion.2
  275.7 1.4 bitcast_dynamic-update-slice_fusion.1
  277.1 6.2 %copy-done.2 = f32[8,1024,512]{2,1,0:T(8,128)} copy-done((f32[8,1024,512]{2,1,0:T(8,128)}, f32[8,1024,512]{2,1,0:T(8,128)S(1)}, u32[]{:S(2)}) %copy-start.2) | copy-done | bytes 16777240
  283.2 2.7 bitcast_dynamic-update-slice_fusion
  (15 shorter events, 3.8 us)
Async XLA Ops:
  6.5 259.2 %all-reduce.4.cloned.1.call-start = ((), (), s32[]{:S(2)}) async-start(), calls=%async_computation | async-start | bytes 4194304 | tf_op jit(solution)/shard_map/psum | solution.py:29
  83.6 48.7 %collective-permute-start = (f32[1024,512]{0,1:T(8,128)S(1)}, f32[1024,512]{0,1:T(8,128)S(1)}, u32[]{:S(2)}, u32[]{:S(2)}) collective-permute-start(f32[1024,512]{0,1:T(8,128)S(1)} %fusion.4), channel_id=1, source_target_pairs={{0,8},{8,0},{16,24},{24,16},{1,9},{9,1},{17,25},{25,17},{2,10},{10... | collective-permute-start | bytes 6291464 | tf_op jit(solution)/shard_map/ppermute | solution.py:18
  132.7 47.0 %collective-permute-start.1 = (f32[1024,512]{0,1:T(8,128)S(1)}, f32[1024,512]{0,1:T(8,128)}, u32[]{:S(2)}, u32[]{:S(2)}) collective-permute-start(f32[1024,512]{0,1:T(8,128)S(1)} %add.57), channel_id=1, source_target_pairs={{0,16},{8,24},{16,0},{24,8},{1,17},{9,25},{17,1},{25,9},{2,18},{10... | collective-permute-start | bytes 6291464 | tf_op jit(solution)/shard_map/ppermute | solution.py:18
  201.1 1.1 copy-start.1
  265.8 1.5 copy-start
  277.1 6.2 %copy-start.2 = (f32[8,1024,512]{2,1,0:T(8,128)}, f32[8,1024,512]{2,1,0:T(8,128)S(1)}, u32[]{:S(2)}) copy-start(f32[8,1024,512]{2,1,0:T(8,128)S(1)} %bitcast_dynamic-update-slice_fusion.1) | copy-start | bytes 50331652
Sparse Core Ops, SparseCore 0:
  202.3 63.4 all-reduce.3
